TPU v7x, 32 devices: a whole 2x2x4 slice. The times are simulated.
32 devices in a mesh: ctx: 16 (over z, x, core), head: 2 (over y).
Axes of the slice: x: 2, y: 2, z: 4, core: 2. Of those that a mesh axis runs over, the one named last changes fastest.
Arguments:
- queries: bfloat16 [4096, 4096], P('ctx', 'head')
- keys: bfloat16 [4096, 1024], P(('ctx', 'head'))
- values: bfloat16 [4096, 1024], P(('ctx', 'head')), may hold values from -6 to 6
- selected: int32 [32, 8, 3], P('ctx', 'head'), may hold values from 0 to 6, as said below
Outputs:
- attended: bfloat16 [4096, 4096], P('ctx', 'head')
Inputs may be any that keep to these rules, and one draw needn't show every extreme that they name: selected[t, g, :] names 3 different blocks of 512 positions that lie before the block of tile t; where fewer than 3 such blocks exist, the remaining entries equal the tile's own block and name nothing more.
All inputs are finite; a program needn't handle non-finite values.
Results may differ from a plain program's by a relative error of at most 0.0041.
Values may be sent and summed in bfloat16 or wider, within the bound.
No kernel may reach another device: no remote copies, remote signals or barrier semaphores. Data moves between devices by JAX's collectives and lax.ppermute only.
A program may use at most 64 MiB of HBM per device.

v0:
```python
import math
import jax
import jax.numpy as jnp
from jax import lax
from jax.sharding import PartitionSpec as P

HD = 128
QH = 32
KVH = 8
BLK = 512
TILE = 128
floor_value = -1e30


def body(queries, keys, values, selected):
    local_rows = queries.shape[0]
    group_count = KVH // lax.axis_size("head")
    per_group = QH // KVH
    score_scale = HD ** (-0.5)
    own_keys, own_values = (
        lax.all_to_all(keys, "head", split_axis=1, concat_axis=0, tiled=True),
        lax.all_to_all(values, "head", split_axis=1, concat_axis=0, tiled=True),
    )
    query_four = queries.reshape(local_rows, group_count, per_group, HD)
    offset = lax.axis_index("ctx") * local_rows
    query_pos = offset + jnp.arange(local_rows, dtype=jnp.int32)
    query_block = query_pos // BLK
    row_select = jnp.repeat(selected, TILE, axis=0)

    def attend(running, key_rows, value_rows, first_row):
        row_count = key_rows.shape[0]
        key_pos = first_row + jnp.arange(row_count, dtype=jnp.int32)
        key_block = key_pos // BLK
        own_part = (key_block[None, :] == query_block[:, None]) & (
            key_pos[None, :] <= query_pos[:, None]
        )
        picked = jnp.any(row_select[:, :, :, None] == key_block[None, None, None, :], axis=2)
        picked = picked & (key_block[None, None, :] != query_block[:, None, None])
        allowed = jnp.transpose(picked | own_part[:, None, :], (1, 0, 2))

        def compute(current):
            running_max, totals, accumulated = current
            scores = (
                jnp.einsum(
                    "qgjd,kgd->gjqk",
                    query_four,
                    key_rows.reshape(row_count, group_count, HD),
                    preferred_element_type=jnp.float32,
                )
                * score_scale
            )
            live_mask = allowed[:, None]
            row_top = jnp.max(jnp.where(live_mask, scores, floor_value), axis=-1)
            newest = jnp.maximum(running_max, row_top)
            weights = jnp.where(live_mask, jnp.exp(scores - newest[..., None]), 0.0)
            factor = jnp.exp(running_max - newest)
            totals = totals * factor + jnp.sum(weights, axis=-1)
            product = jnp.einsum(
                "gjqk,kgd->gjqd",
                weights.astype(jnp.bfloat16),
                value_rows.reshape(row_count, group_count, HD),
                preferred_element_type=jnp.float32,
            )
            accumulated = accumulated * factor[..., None] + product
            return (newest, totals, accumulated)

        def keep_running(current):
            return current

        needed = jnp.any(allowed)
        return lax.cond(needed, compute, keep_running, running)

    start_max = jnp.full((group_count, per_group, local_rows), floor_value, jnp.float32)
    start_totals = jnp.zeros((group_count, per_group, local_rows), jnp.float32)
    start_accumulated = jnp.zeros((group_count, per_group, local_rows, HD), jnp.float32)
    key_piece = lax.all_gather(own_keys, "ctx", axis=0, tiled=True)
    value_piece = lax.all_gather(own_values, "ctx", axis=0, tiled=True)
    row_count = key_piece.shape[0]
    step_rows = math.gcd(row_count, 512)

    def loop_body(block_index, current):
        key_part = lax.dynamic_slice_in_dim(key_piece, block_index * step_rows, step_rows, 0)
        value_part = lax.dynamic_slice_in_dim(value_piece, block_index * step_rows, step_rows, 0)
        return attend(current, key_part, value_part, block_index * step_rows)

    running_max, totals, accumulated = lax.fori_loop(
        0, row_count // step_rows, loop_body, (start_max, start_totals, start_accumulated)
    )
    mixed = accumulated / totals[..., None]
    return (
        jnp.transpose(mixed, (2, 0, 1, 3))
        .reshape(local_rows, group_count * per_group * HD)
        .astype(jnp.bfloat16)
    )


def solution(mesh):
    placed = (
        P("ctx", "head"),
        P(("ctx", "head"), None),
        P(("ctx", "head"), None),
        P("ctx", "head", None),
    )
    return jax.shard_map(
        body, mesh=mesh, in_specs=placed, out_specs=P("ctx", "head"), check_vma=False
    )
```

profile of v0, /device:TPU:27, one launch (start us, length us, event | category | flops | bytes accessed | tf_op | source)
XLA Modules:
  0.0 254.5 jit_solution(11256422979810992226)
XLA Ops:
  7.8 6.7 %all_to_all.38 = bf16[128,2,512]{0,2,1:T(8,128)(2,1)S(1)} all-to-all(bf16[128,2,512]{0,2,1:T(8,128)(2,1)S(1)} %bitcast.60), channel_id=1, replica_groups=mesh['ctx'=16,'head'=2] {'head'}, dimensions={1} | all-to-all | bytes 524288 | tf_op jit(solution)/shard_map/all_to_all | solution.py:21
  16.5 6.4 %all_to_all.39 = bf16[128,2,512]{0,2,1:T(8,128)(2,1)S(1)} all-to-all(bf16[128,2,512]{0,2,1:T(8,128)(2,1)S(1)} %bitcast.61), channel_id=1, replica_groups=mesh['ctx'=16,'head'=2] {'head'}, dimensions={1} | all-to-all | bytes 524288 | tf_op jit(solution)/shard_map/all_to_all | solution.py:22
  25.8 39.4 %all-gather.3.cloned.1.call-done = bf16[4096,512]{1,0:T(8,128)(2,1)} async-done(((bf16[256,512]{1,0:T(8,128)(2,1)}), bf16[4096,512]{1,0:T(8,128)(2,1)}) %all-gather.3.cloned.1.call-update) | async-done | bytes 4194320 | tf_op jit(solution)/shard_map/all_gather | solution.py:76
  65.2 6.4 %copy.69 = bf16[4096,512]{0,1:T(8,128)(2,1)} copy(bf16[4096,512]{1,0:T(8,128)(2,1)} %all-gather.3.cloned.1.call-done) | data formatting | bytes 8388608
  71.6 44.8 %all-gather.5.cloned.1.call-done = bf16[4096,512]{1,0:T(8,128)(2,1)} async-done(((bf16[256,512]{1,0:T(8,128)(2,1)}), bf16[4096,512]{1,0:T(8,128)(2,1)}) %all-gather.5.cloned.1.call-update) | async-done | bytes 4194320 | tf_op jit(solution)/shard_map/all_gather | solution.py:77
  116.4 6.5 %copy.71 = bf16[4096,512]{0,1:T(8,128)(2,1)} copy(bf16[4096,512]{1,0:T(8,128)(2,1)} %all-gather.5.cloned.1.call-done) | data formatting | bytes 8388608
  122.9 1.6 broadcast_in_dim.69
  124.5 118.8 %while.21 = (s32[]{:T(128)}, f32[4,4,256]{2,1,0:T(4,128)S(1)}, f32[4,4,256]{2,1,0:T(4,128)S(1)}, f32[4,4,256,128]{3,2,1,0:T(8,128)}, bf16[4096,512]{0,1:T(8,128)...) while((s32[]{:T(128)}, f32[4,4,256]{2,1,0:T(4,128)S(1)}, ...), condition=%wide.region_7.8_spmd.clone.clone, body=%wide.region_0.7_spmd.clone.clone.sunk | while | flops 1103646720 | bytes 56711624 | solution.py:86
  128.2 11.1 %conditional.4 = ((f32[4,4,256]{2,1,0:T(4,128)S(1)}, f32[4,4,256]{2,1,0:T(4,128)S(1)}, f32[4,4,256,128]{3,2,1,0:T(8,128)})) conditional(s32[]{:T(128)} %convert_element_type.38, (f32[4,4,256]{2,1,0:T(4,128)S(1)}, f32[4,4,256]{2,1,0:T(4,128)S(1)}, f32[4,4,256,128]{3,2,1,0:T(8,128)}) %tuple.84, (pred[256,512]{0,1:T(8,128)(4,1)S(1)}, ...), branch_computations={%region_3.3_spmd, %region_4.6_spmd} | conditional | flops 1098915840 | bytes 54526076 | solution.py:71
  130.9 1.9 fusion.6
  132.8 1.8 fusion.10
  134.6 3.3 %multiply_add_fusion = f32[4,4,256,128]{3,2,1,0:T(8,128)S(1)} fusion(f32[4,4,256,128]{3,2,1,0:T(8,128)S(1)} %copy-done, bf16[512,4,128,1]{0,2,3,1:T(8,128)(2,1)S(1)} %bitcast.53, f32[4,512,256,4]{2,1,3,0:T(8,128)S(1)} %get-tuple-element.534, f32[4,4,256]{2,1,0:T(4,128)S(1)} %max.5, pred[4,256,512]{1,2,0:T(8,128)(4,1)S(1)} %and_or_fusion, ...), kind=kOutput, calls=%fused_computation.15 | convolution fusion | flops 546308096 | bytes 13664256 | tf_op jit(solution)/shard_map/while/body/eval_jaxpr/cond/branch_1_fun/gjqk,kgd->gjqd/dot_general | solution.py:58
  138.0 1.3 copy-done.1
  143.0 11.1 %conditional.4 = ((f32[4,4,256]{2,1,0:T(4,128)S(1)}, f32[4,4,256]{2,1,0:T(4,128)S(1)}, f32[4,4,256,128]{3,2,1,0:T(8,128)})) conditional(s32[]{:T(128)} %convert_element_type.38, (f32[4,4,256]{2,1,0:T(4,128)S(1)}, f32[4,4,256]{2,1,0:T(4,128)S(1)}, f32[4,4,256,128]{3,2,1,0:T(8,128)}) %tuple.84, (pred[256,512]{0,1:T(8,128)(4,1)S(1)}, ...), branch_computations={%region_3.3_spmd, %region_4.6_spmd} | conditional | flops 1098915840 | bytes 54526076 | solution.py:71
  145.7 1.9 fusion.6
  147.6 1.8 fusion.10
  149.5 3.3 %multiply_add_fusion = f32[4,4,256,128]{3,2,1,0:T(8,128)S(1)} fusion(f32[4,4,256,128]{3,2,1,0:T(8,128)S(1)} %copy-done, bf16[512,4,128,1]{0,2,3,1:T(8,128)(2,1)S(1)} %bitcast.53, f32[4,512,256,4]{2,1,3,0:T(8,128)S(1)} %get-tuple-element.534, f32[4,4,256]{2,1,0:T(4,128)S(1)} %max.5, pred[4,256,512]{1,2,0:T(8,128)(4,1)S(1)} %and_or_fusion, ...), kind=kOutput, calls=%fused_computation.15 | convolution fusion | flops 546308096 | bytes 13664256 | tf_op jit(solution)/shard_map/while/body/eval_jaxpr/cond/branch_1_fun/gjqk,kgd->gjqd/dot_general | solution.py:58
  152.8 1.3 copy-done.1
  157.9 11.1 %conditional.4 = ((f32[4,4,256]{2,1,0:T(4,128)S(1)}, f32[4,4,256]{2,1,0:T(4,128)S(1)}, f32[4,4,256,128]{3,2,1,0:T(8,128)})) conditional(s32[]{:T(128)} %convert_element_type.38, (f32[4,4,256]{2,1,0:T(4,128)S(1)}, f32[4,4,256]{2,1,0:T(4,128)S(1)}, f32[4,4,256,128]{3,2,1,0:T(8,128)}) %tuple.84, (pred[256,512]{0,1:T(8,128)(4,1)S(1)}, ...), branch_computations={%region_3.3_spmd, %region_4.6_spmd} | conditional | flops 1098915840 | bytes 54526076 | solution.py:71
  160.5 1.9 fusion.6
  162.5 1.8 fusion.10
  164.3 3.3 %multiply_add_fusion = f32[4,4,256,128]{3,2,1,0:T(8,128)S(1)} fusion(f32[4,4,256,128]{3,2,1,0:T(8,128)S(1)} %copy-done, bf16[512,4,128,1]{0,2,3,1:T(8,128)(2,1)S(1)} %bitcast.53, f32[4,512,256,4]{2,1,3,0:T(8,128)S(1)} %get-tuple-element.534, f32[4,4,256]{2,1,0:T(4,128)S(1)} %max.5, pred[4,256,512]{1,2,0:T(8,128)(4,1)S(1)} %and_or_fusion, ...), kind=kOutput, calls=%fused_computation.15 | convolution fusion | flops 546308096 | bytes 13664256 | tf_op jit(solution)/shard_map/while/body/eval_jaxpr/cond/branch_1_fun/gjqk,kgd->gjqd/dot_general | solution.py:58
  167.7 1.3 copy-done.1
  172.7 11.1 %conditional.4 = ((f32[4,4,256]{2,1,0:T(4,128)S(1)}, f32[4,4,256]{2,1,0:T(4,128)S(1)}, f32[4,4,256,128]{3,2,1,0:T(8,128)})) conditional(s32[]{:T(128)} %convert_element_type.38, (f32[4,4,256]{2,1,0:T(4,128)S(1)}, f32[4,4,256]{2,1,0:T(4,128)S(1)}, f32[4,4,256,128]{3,2,1,0:T(8,128)}) %tuple.84, (pred[256,512]{0,1:T(8,128)(4,1)S(1)}, ...), branch_computations={%region_3.3_spmd, %region_4.6_spmd} | conditional | flops 1098915840 | bytes 54526076 | solution.py:71
  175.4 1.9 fusion.6
  177.3 1.8 fusion.10
  179.2 3.3 %multiply_add_fusion = f32[4,4,256,128]{3,2,1,0:T(8,128)S(1)} fusion(f32[4,4,256,128]{3,2,1,0:T(8,128)S(1)} %copy-done, bf16[512,4,128,1]{0,2,3,1:T(8,128)(2,1)S(1)} %bitcast.53, f32[4,512,256,4]{2,1,3,0:T(8,128)S(1)} %get-tuple-element.534, f32[4,4,256]{2,1,0:T(4,128)S(1)} %max.5, pred[4,256,512]{1,2,0:T(8,128)(4,1)S(1)} %and_or_fusion, ...), kind=kOutput, calls=%fused_computation.15 | convolution fusion | flops 546308096 | bytes 13664256 | tf_op jit(solution)/shard_map/while/body/eval_jaxpr/cond/branch_1_fun/gjqk,kgd->gjqd/dot_general | solution.py:58
  182.5 1.3 copy-done.1
  187.6 11.1 %conditional.4 = ((f32[4,4,256]{2,1,0:T(4,128)S(1)}, f32[4,4,256]{2,1,0:T(4,128)S(1)}, f32[4,4,256,128]{3,2,1,0:T(8,128)})) conditional(s32[]{:T(128)} %convert_element_type.38, (f32[4,4,256]{2,1,0:T(4,128)S(1)}, f32[4,4,256]{2,1,0:T(4,128)S(1)}, f32[4,4,256,128]{3,2,1,0:T(8,128)}) %tuple.84, (pred[256,512]{0,1:T(8,128)(4,1)S(1)}, ...), branch_computations={%region_3.3_spmd, %region_4.6_spmd} | conditional | flops 1098915840 | bytes 54526076 | solution.py:71
  190.2 1.9 fusion.6
  192.2 1.8 fusion.10
  194.0 3.3 %multiply_add_fusion = f32[4,4,256,128]{3,2,1,0:T(8,128)S(1)} fusion(f32[4,4,256,128]{3,2,1,0:T(8,128)S(1)} %copy-done, bf16[512,4,128,1]{0,2,3,1:T(8,128)(2,1)S(1)} %bitcast.53, f32[4,512,256,4]{2,1,3,0:T(8,128)S(1)} %get-tuple-element.534, f32[4,4,256]{2,1,0:T(4,128)S(1)} %max.5, pred[4,256,512]{1,2,0:T(8,128)(4,1)S(1)} %and_or_fusion, ...), kind=kOutput, calls=%fused_computation.15 | convolution fusion | flops 546308096 | bytes 13664256 | tf_op jit(solution)/shard_map/while/body/eval_jaxpr/cond/branch_1_fun/gjqk,kgd->gjqd/dot_general | solution.py:58
  202.4 11.1 %conditional.4 = ((f32[4,4,256]{2,1,0:T(4,128)S(1)}, f32[4,4,256]{2,1,0:T(4,128)S(1)}, f32[4,4,256,128]{3,2,1,0:T(8,128)})) conditional(s32[]{:T(128)} %convert_element_type.38, (f32[4,4,256]{2,1,0:T(4,128)S(1)}, f32[4,4,256]{2,1,0:T(4,128)S(1)}, f32[4,4,256,128]{3,2,1,0:T(8,128)}) %tuple.84, (pred[256,512]{0,1:T(8,128)(4,1)S(1)}, ...), branch_computations={%region_3.3_spmd, %region_4.6_spmd} | conditional | flops 1098915840 | bytes 54526076 | solution.py:71
  205.1 1.9 fusion.6
  207.0 1.8 fusion.10
  208.9 3.3 %multiply_add_fusion = f32[4,4,256,128]{3,2,1,0:T(8,128)S(1)} fusion(f32[4,4,256,128]{3,2,1,0:T(8,128)S(1)} %copy-done, bf16[512,4,128,1]{0,2,3,1:T(8,128)(2,1)S(1)} %bitcast.53, f32[4,512,256,4]{2,1,3,0:T(8,128)S(1)} %get-tuple-element.534, f32[4,4,256]{2,1,0:T(4,128)S(1)} %max.5, pred[4,256,512]{1,2,0:T(8,128)(4,1)S(1)} %and_or_fusion, ...), kind=kOutput, calls=%fused_computation.15 | convolution fusion | flops 546308096 | bytes 13664256 | tf_op jit(solution)/shard_map/while/body/eval_jaxpr/cond/branch_1_fun/gjqk,kgd->gjqd/dot_general | solution.py:58
  217.3 11.1 %conditional.4 = ((f32[4,4,256]{2,1,0:T(4,128)S(1)}, f32[4,4,256]{2,1,0:T(4,128)S(1)}, f32[4,4,256,128]{3,2,1,0:T(8,128)})) conditional(s32[]{:T(128)} %convert_element_type.38, (f32[4,4,256]{2,1,0:T(4,128)S(1)}, f32[4,4,256]{2,1,0:T(4,128)S(1)}, f32[4,4,256,128]{3,2,1,0:T(8,128)}) %tuple.84, (pred[256,512]{0,1:T(8,128)(4,1)S(1)}, ...), branch_computations={%region_3.3_spmd, %region_4.6_spmd} | conditional | flops 1098915840 | bytes 54526076 | solution.py:71
  219.9 1.9 fusion.6
  221.9 1.8 fusion.10
  223.7 3.3 %multiply_add_fusion = f32[4,4,256,128]{3,2,1,0:T(8,128)S(1)} fusion(f32[4,4,256,128]{3,2,1,0:T(8,128)S(1)} %copy-done, bf16[512,4,128,1]{0,2,3,1:T(8,128)(2,1)S(1)} %bitcast.53, f32[4,512,256,4]{2,1,3,0:T(8,128)S(1)} %get-tuple-element.534, f32[4,4,256]{2,1,0:T(4,128)S(1)} %max.5, pred[4,256,512]{1,2,0:T(8,128)(4,1)S(1)} %and_or_fusion, ...), kind=kOutput, calls=%fused_computation.15 | convolution fusion | flops 546308096 | bytes 13664256 | tf_op jit(solution)/shard_map/while/body/eval_jaxpr/cond/branch_1_fun/gjqk,kgd->gjqd/dot_general | solution.py:58
  227.1 1.3 copy-done.1
  232.1 11.1 %conditional.4 = ((f32[4,4,256]{2,1,0:T(4,128)S(1)}, f32[4,4,256]{2,1,0:T(4,128)S(1)}, f32[4,4,256,128]{3,2,1,0:T(8,128)})) conditional(s32[]{:T(128)} %convert_element_type.38, (f32[4,4,256]{2,1,0:T(4,128)S(1)}, f32[4,4,256]{2,1,0:T(4,128)S(1)}, f32[4,4,256,128]{3,2,1,0:T(8,128)}) %tuple.84, (pred[256,512]{0,1:T(8,128)(4,1)S(1)}, ...), branch_computations={%region_3.3_spmd, %region_4.6_spmd} | conditional | flops 1098915840 | bytes 54526076 | solution.py:71
  234.8 1.9 fusion.6
  236.7 1.8 fusion.10
  238.6 3.3 %multiply_add_fusion = f32[4,4,256,128]{3,2,1,0:T(8,128)S(1)} fusion(f32[4,4,256,128]{3,2,1,0:T(8,128)S(1)} %copy-done, bf16[512,4,128,1]{0,2,3,1:T(8,128)(2,1)S(1)} %bitcast.53, f32[4,512,256,4]{2,1,3,0:T(8,128)S(1)} %get-tuple-element.534, f32[4,4,256]{2,1,0:T(4,128)S(1)} %max.5, pred[4,256,512]{1,2,0:T(8,128)(4,1)S(1)} %and_or_fusion, ...), kind=kOutput, calls=%fused_computation.15 | convolution fusion | flops 546308096 | bytes 13664256 | tf_op jit(solution)/shard_map/while/body/eval_jaxpr/cond/branch_1_fun/gjqk,kgd->gjqd/dot_general | solution.py:58
  241.9 1.3 copy-done.1
  243.3 1.9 fusion.24
  246.0 1.6 convert_element_type.27
  (170 shorter events, 55.1 us)
Async XLA Ops:
  6.5 18.1 %copy-start.2 = (bf16[256,2048]{1,0:T(8,128)(2,1)S(1)}, bf16[256,2048]{1,0:T(8,128)(2,1)}, u32[]{:S(2)}) copy-start(bf16[256,2048]{1,0:T(8,128)(2,1)} %param.8) | copy-start | bytes 3145732
  6.5 58.6 %all-gather.3.cloned.1.call-start = ((), (), s32[]{:S(2)}) async-start(), calls=%async_computation.2 | async-start | bytes 4456448 | tf_op jit(solution)/shard_map/all_gather | solution.py:76
  15.4 101.1 %all-gather.5.cloned.1.call-start = ((), (), s32[]{:S(2)}) async-start(), calls=%async_computation.3 | async-start | bytes 4456448 | tf_op jit(solution)/shard_map/all_gather | solution.py:77
  132.8 1.9 copy-start
  138.0 1.4 copy-start.1
  147.6 1.9 copy-start
  152.8 1.4 copy-start.1
  162.5 1.9 copy-start
  167.7 1.4 copy-start.1
  177.3 1.9 copy-start
  182.5 1.4 copy-start.1
  192.1 1.9 copy-start
  197.4 1.4 copy-start.1
  207.0 1.9 copy-start
  212.2 1.4 copy-start.1
  221.8 1.9 copy-start
  227.1 1.4 copy-start.1
  236.7 1.9 copy-start
  241.9 1.4 copy-start.1
Sparse Core Ops, SparseCore 0:
  15.5 49.6 all-gather.2
  67.3 49.0 all-gather.4
where the time goes:
time: 255 us; the launch traced here: 254 us
  waiting for transfers between devices  84.2 us (33%)
  local copies, waits for them, and re-layouts  56.3 us (22%)
  matrix products  41.6 us (16%)
  other arithmetic  39.5 us (15%)
  between operations  13.5 us (5%)
  blocking collectives  13.1 us (5%)
  loops' own time  6.12 us (2%)
    all_gather x1, waiting for transfers between devices, body(): value_piece = lax.all_gather(own_values, 'ctx', axis=0, tiled=True)  44.8 us
    all_gather x1, waiting for transfers between devices, body(): key_piece = lax.all_gather(own_keys, 'ctx', axis=0, tiled=True)  39.4 us
    dot_general x8, matrix products, compute(): jnp.einsum('gjqk,kgd->gjqd', weights.astype(jnp.bfloat16), value_rows.res...  26.6 us
    unnamed x9, local copies, waits for them, and re-layouts  17.2 us
    dot_general x8, matrix products, compute(): jnp.einsum('qgjd,kgd->gjqk', query_four, key_rows.reshape(row_count, grou...  15.1 us
    reduce_sum x8, other arithmetic, compute(): totals = totals * factor + jnp.sum(weights, axis=-1)  14.7 us
    cond x40, local copies, waits for them, and re-layouts  10.8 us
    dynamic_slice x8, local copies, waits for them, and re-layouts, loop_body(): lax.dynamic_slice_in_dim(value_piece, block_index * step_rows, step_rows, 0)  10.2 us
  transfers between devices with their start and end apart: 2, of which 2 were waited for; matrix products, arithmetic and copies ran while one was open for 4% of the time, Pallas kernels for 0%

commit v1 on v0

--- a/solution.py
+++ b/solution.py
@@ -10,6 +10,28 @@
 BLK = 512
 TILE = 128
 floor_value = -1e30
+
+
+def laid_out(blocks, dim):
+    lengths = list(blocks.shape[1:])
+    lengths[dim] *= blocks.shape[0]
+    return jnp.moveaxis(blocks, 0, dim).reshape(lengths)
+
+
+def ring_gather(x, axis, dim):
+    size = lax.axis_size(axis)
+    pairs = [(i, (i + 1) % size) for i in range(size)]
+    back = [(b, a) for a, b in pairs]
+    lower, upper = ([], [])
+    for step in range(size - 1):
+        if step % 2 == 0:
+            lower.append(lax.ppermute(lower[-1] if lower else x, axis, pairs))
+        else:
+            upper.append(lax.ppermute(upper[-1] if upper else x, axis, back))
+    blocks = jnp.stack([*lower[::-1], x, *upper])
+    shift = lax.axis_index(axis) - len(lower)
+    blocks = blocks[(jnp.arange(size) - shift) % size]
+    return laid_out(blocks, dim)
 
 
 def body(queries, keys, values, selected):
@@ -74,7 +96,7 @@
     start_totals = jnp.zeros((group_count, per_group, local_rows), jnp.float32)
     start_accumulated = jnp.zeros((group_count, per_group, local_rows, HD), jnp.float32)
     key_piece = lax.all_gather(own_keys, "ctx", axis=0, tiled=True)
-    value_piece = lax.all_gather(own_values, "ctx", axis=0, tiled=True)
+    value_piece = ring_gather(own_values, "ctx", 0)
     row_count = key_piece.shape[0]
     step_rows = math.gcd(row_count, 512)
 

time: 255 us -> 272 us (1.067)
  waiting for transfers between devices: 84.2 us -> 36.6 us
  starting transfers between devices: 0.04 us -> 39.6 us
  local copies, waits for them, and re-layouts: 56.3 us -> 80.5 us
    all_gather x1 -> x0, waiting for transfers between devices: 44.8 us -> none  [body(): value_piece = lax.all_gather(own_values, 'ctx', axis=0, tiled=True)]
    ppermute x0 -> x15, starting transfers between devices: none -> 39.6 us  [the longest x8 39.5 us: ring_gather(): lower.append(lax.ppermute(lower[-1] if lower else x, axis, pairs))]
    all_gather x1, waiting for transfers between devices: 39.4 us -> 0.01 us  [body(): key_piece = lax.all_gather(own_keys, 'ctx', axis=0, tiled=True)]
    ppermute x0 -> x15, waiting for transfers between devices: none -> 36.5 us  [the longest x8 29.8 us: ring_gather(): lower.append(lax.ppermute(lower[-1] if lower else x, axis, pairs))]
    unnamed x9 -> x38, local copies, waits for them, and re-layouts: 17.2 us -> 36.6 us
    gather x0 -> x1, local copies, waits for them, and re-layouts: none -> 4.98 us  [ring_gather(): blocks = blocks[(jnp.arange(size) - shift) % size]]
    another operation x8 -> x9, local copies, waits for them, and re-layouts: 7.71 us -> 8.48 us
  transfers between devices with their start and end apart: 2 -> 16, of which waited for: 2 -> 12; matrix products, arithmetic and copies ran while one was open for 4% -> 13% of each run, Pallas kernels for 0% -> 0%
where the time goes in v1:
time: 272 us; the launch traced here: 271 us
  local copies, waits for them, and re-layouts  80.5 us (30%)
  matrix products  41.6 us (15%)
  other arithmetic  39.7 us (15%)
  starting transfers between devices  39.6 us (15%)
  waiting for transfers between devices  36.6 us (13%)
  between operations  13.6 us (5%)
  blocking collectives  13.1 us (5%)
  loops' own time  6.07 us (2%)
    ppermute x8, starting transfers between devices, ring_gather(): lower.append(lax.ppermute(lower[-1] if lower else x, axis, pairs))  39.5 us
    unnamed x38, local copies, waits for them, and re-layouts  36.6 us
    ppermute x8, waiting for transfers between devices, ring_gather(): lower.append(lax.ppermute(lower[-1] if lower else x, axis, pairs))  29.8 us
    dot_general x8, matrix products, compute(): jnp.einsum('gjqk,kgd->gjqd', weights.astype(jnp.bfloat16), value_rows.res...  26.6 us
    dot_general x8, matrix products, compute(): jnp.einsum('qgjd,kgd->gjqk', query_four, key_rows.reshape(row_count, grou...  15 us
    reduce_sum x8, other arithmetic, compute(): totals = totals * factor + jnp.sum(weights, axis=-1)  14.7 us
    cond x40, local copies, waits for them, and re-layouts  10.6 us
    dynamic_slice x8, local copies, waits for them, and re-layouts, loop_body(): lax.dynamic_slice_in_dim(value_piece, block_index * step_rows, step_rows, 0)  10.2 us
  transfers between devices with their start and end apart: 16, of which 12 were waited for; matrix products, arithmetic and copies ran while one was open for 13% of the time, Pallas kernels for 0%

profile of v1, /device:TPU:27, one launch (start us, length us, event | category | flops | bytes accessed | tf_op | source)
XLA Modules:
  0.0 270.8 jit_solution(15227981520309815129)
XLA Ops:
  7.7 6.7 %all_to_all.38 = bf16[128,2,512]{0,2,1:T(8,128)(2,1)S(1)} all-to-all(bf16[128,2,512]{0,2,1:T(8,128)(2,1)S(1)} %bitcast.99), channel_id=1, replica_groups=mesh['ctx'=16,'head'=2] {'head'}, dimensions={1} | all-to-all | bytes 524288 | tf_op jit(solution)/shard_map/all_to_all | solution.py:43
  16.4 6.4 %all_to_all.39 = bf16[128,2,512]{0,2,1:T(8,128)(2,1)S(1)} all-to-all(bf16[128,2,512]{0,2,1:T(8,128)(2,1)S(1)} %bitcast.100), channel_id=1, replica_groups=mesh['ctx'=16,'head'=2] {'head'}, dimensions={1} | all-to-all | bytes 524288 | tf_op jit(solution)/shard_map/all_to_all | solution.py:44
  23.0 2.7 collective-permute-start
  25.7 8.7 %collective-permute-done = bf16[256,512]{1,0:T(8,128)(2,1)S(1)} collective-permute-done((bf16[256,512]{1,0:T(8,128)(2,1)S(1)}, bf16[256,512]{1,0:T(8,128)(2,1)S(1)}, u32[]{:S(2)}, u32[]{:S(2)}) %collective-permute-start) | collective-permute-done | bytes 262176 | tf_op jit(solution)/shard_map/ppermute | solution.py:28
  34.3 5.2 %collective-permute-start.1 = (bf16[256,512]{1,0:T(8,128)(2,1)S(1)}, bf16[256,512]{1,0:T(8,128)(2,1)S(1)}, u32[]{:S(2)}, u32[]{:S(2)}) collective-permute-start(bf16[256,512]{1,0:T(8,128)(2,1)S(1)} %collective-permute-done), channel_id=1, source_target_pairs={{0,2},{2,4},{4,6},{6,8},{8,10},{10,12},{12,14},{14,16},{16,18},{18... | collective-permute-start | bytes 786440 | tf_op jit(solution)/shard_map/ppermute | solution.py:28
  39.5 3.3 %collective-permute-done.1 = bf16[256,512]{1,0:T(8,128)(2,1)S(1)} collective-permute-done((bf16[256,512]{1,0:T(8,128)(2,1)S(1)}, bf16[256,512]{1,0:T(8,128)(2,1)S(1)}, u32[]{:S(2)}, u32[]{:S(2)}) %collective-permute-start.1) | collective-permute-done | bytes 262176 | tf_op jit(solution)/shard_map/ppermute | solution.py:28
  42.8 5.3 %collective-permute-start.2 = (bf16[256,512]{1,0:T(8,128)(2,1)S(1)}, bf16[256,512]{1,0:T(8,128)(2,1)S(1)}, u32[]{:S(2)}, u32[]{:S(2)}) collective-permute-start(bf16[256,512]{1,0:T(8,128)(2,1)S(1)} %collective-permute-done.1), channel_id=1, source_target_pairs={{0,2},{2,4},{4,6},{6,8},{8,10},{10,12},{12,14},{14,16},{16,18},{18... | collective-permute-start | bytes 786440 | tf_op jit(solution)/shard_map/ppermute | solution.py:28
  49.4 7.5 %collective-permute-done.2 = bf16[256,512]{1,0:T(8,128)(2,1)S(1)} collective-permute-done((bf16[256,512]{1,0:T(8,128)(2,1)S(1)}, bf16[256,512]{1,0:T(8,128)(2,1)S(1)}, u32[]{:S(2)}, u32[]{:S(2)}) %collective-permute-start.2) | collective-permute-done | bytes 262176 | tf_op jit(solution)/shard_map/ppermute | solution.py:28
  56.9 5.2 %collective-permute-start.3 = (bf16[256,512]{1,0:T(8,128)(2,1)S(1)}, bf16[256,512]{1,0:T(8,128)(2,1)S(1)}, u32[]{:S(2)}, u32[]{:S(2)}) collective-permute-start(bf16[256,512]{1,0:T(8,128)(2,1)S(1)} %collective-permute-done.2), channel_id=1, source_target_pairs={{0,2},{2,4},{4,6},{6,8},{8,10},{10,12},{12,14},{14,16},{16,18},{18... | collective-permute-start | bytes 786440 | tf_op jit(solution)/shard_map/ppermute | solution.py:28
  62.1 4.7 %collective-permute-done.3 = bf16[256,512]{1,0:T(8,128)(2,1)S(1)} collective-permute-done((bf16[256,512]{1,0:T(8,128)(2,1)S(1)}, bf16[256,512]{1,0:T(8,128)(2,1)S(1)}, u32[]{:S(2)}, u32[]{:S(2)}) %collective-permute-start.3) | collective-permute-done | bytes 262176 | tf_op jit(solution)/shard_map/ppermute | solution.py:28
  66.9 5.3 %collective-permute-start.4 = (bf16[256,512]{1,0:T(8,128)(2,1)S(1)}, bf16[256,512]{1,0:T(8,128)(2,1)S(1)}, u32[]{:S(2)}, u32[]{:S(2)}) collective-permute-start(bf16[256,512]{1,0:T(8,128)(2,1)S(1)} %collective-permute-done.3), channel_id=1, source_target_pairs={{0,2},{2,4},{4,6},{6,8},{8,10},{10,12},{12,14},{14,16},{16,18},{18... | collective-permute-start | bytes 786440 | tf_op jit(solution)/shard_map/ppermute | solution.py:28
  72.1 2.2 collective-permute-done.10
  76.0 5.3 %collective-permute-start.5 = (bf16[256,512]{1,0:T(8,128)(2,1)S(1)}, bf16[256,512]{1,0:T(8,128)(2,1)S(1)}, u32[]{:S(2)}, u32[]{:S(2)}) collective-permute-start(bf16[256,512]{1,0:T(8,128)(2,1)S(1)} %collective-permute-done.4), channel_id=1, source_target_pairs={{0,2},{2,4},{4,6},{6,8},{8,10},{10,12},{12,14},{14,16},{16,18},{18... | collective-permute-start | bytes 786440 | tf_op jit(solution)/shard_map/ppermute | solution.py:28
  84.6 5.3 %collective-permute-start.6 = (bf16[256,512]{1,0:T(8,128)(2,1)S(1)}, bf16[256,512]{1,0:T(8,128)(2,1)}, u32[]{:S(2)}, u32[]{:S(2)}) collective-permute-start(bf16[256,512]{1,0:T(8,128)(2,1)S(1)} %collective-permute-done.5), channel_id=1, source_target_pairs={{0,2},{2,4},{4,6},{6,8},{8,10},{10,12},{12,14},{14,16},{16,18},{18... | collective-permute-start | bytes 786440 | tf_op jit(solution)/shard_map/ppermute | solution.py:28
  93.2 5.3 %collective-permute-start.7 = (bf16[256,512]{1,0:T(8,128)(2,1)}, bf16[256,512]{1,0:T(8,128)(2,1)}, u32[]{:S(2)}, u32[]{:S(2)}) collective-permute-start(bf16[256,512]{1,0:T(8,128)(2,1)} %collective-permute-done.6), channel_id=1, source_target_pairs={{0,2},{2,4},{4,6},{6,8},{8,10},{10,12},{12,14},{14,16},{16,18},{18... | collective-permute-start | bytes 786440 | tf_op jit(solution)/shard_map/ppermute | solution.py:28
  121.4 5.0 %gather_fusion = bf16[16,256,512]{2,1,0:T(8,128)(2,1)} fusion(bf16[16,256,512]{2,1,0:T(8,128)(2,1)} %bitcast_dynamic-update-slice_fusion, s32[1024]{0:T(1024)S(1)} %pad_clamp_fusion), kind=kCustom, calls=%fused_computation | custom fusion | bytes 8388672 | tf_op jit(solution)/shard_map/gather | solution.py:33
  126.4 6.5 %copy.88 = bf16[4096,512]{0,1:T(8,128)(2,1)} copy(bf16[4096,512]{1,0:T(8,128)(2,1)} %bitcast.88) | data formatting | bytes 8388608
  132.9 6.4 %copy.86 = bf16[4096,512]{0,1:T(8,128)(2,1)} copy(bf16[4096,512]{1,0:T(8,128)(2,1)} %all-gather.2.cloned.1.call-done) | data formatting | bytes 8388608
  140.9 118.7 %while.21 = (s32[]{:T(128)}, f32[4,4,256]{2,1,0:T(4,128)S(1)}, f32[4,4,256]{2,1,0:T(4,128)S(1)}, f32[4,4,256,128]{3,2,1,0:T(8,128)}, bf16[4096,512]{0,1:T(8,128)...) while((s32[]{:T(128)}, f32[4,4,256]{2,1,0:T(4,128)S(1)}, ...), condition=%wide.region_7.8_spmd.clone.clone, body=%wide.region_0.7_spmd.clone.clone.sunk | while | flops 1103646720 | bytes 56711624 | solution.py:108
  144.6 11.1 %conditional.4 = ((f32[4,4,256]{2,1,0:T(4,128)S(1)}, f32[4,4,256]{2,1,0:T(4,128)S(1)}, f32[4,4,256,128]{3,2,1,0:T(8,128)})) conditional(s32[]{:T(128)} %convert_element_type.38, (f32[4,4,256]{2,1,0:T(4,128)S(1)}, f32[4,4,256]{2,1,0:T(4,128)S(1)}, f32[4,4,256,128]{3,2,1,0:T(8,128)}) %tuple.85, (pred[256,512]{0,1:T(8,128)(4,1)S(1)}, ...), branch_computations={%region_3.3_spmd, %region_4.6_spmd} | conditional | flops 1098915840 | bytes 54526076 | solution.py:93
  147.3 1.9 fusion.6
  149.2 1.8 fusion.10
  151.1 3.3 %multiply_add_fusion = f32[4,4,256,128]{3,2,1,0:T(8,128)S(1)} fusion(f32[4,4,256,128]{3,2,1,0:T(8,128)S(1)} %copy-done, bf16[512,4,128,1]{0,2,3,1:T(8,128)(2,1)S(1)} %bitcast.89, f32[4,512,256,4]{2,1,3,0:T(8,128)S(1)} %get-tuple-element.543, f32[4,4,256]{2,1,0:T(4,128)S(1)} %max.5, pred[4,256,512]{1,2,0:T(8,128)(4,1)S(1)} %and_or_fusion, ...), kind=kOutput, calls=%fused_computation.16 | convolution fusion | flops 546308096 | bytes 13664256 | tf_op jit(solution)/shard_map/while/body/eval_jaxpr/cond/branch_1_fun/gjqk,kgd->gjqd/dot_general | solution.py:80
  159.4 11.1 %conditional.4 = ((f32[4,4,256]{2,1,0:T(4,128)S(1)}, f32[4,4,256]{2,1,0:T(4,128)S(1)}, f32[4,4,256,128]{3,2,1,0:T(8,128)})) conditional(s32[]{:T(128)} %convert_element_type.38, (f32[4,4,256]{2,1,0:T(4,128)S(1)}, f32[4,4,256]{2,1,0:T(4,128)S(1)}, f32[4,4,256,128]{3,2,1,0:T(8,128)}) %tuple.85, (pred[256,512]{0,1:T(8,128)(4,1)S(1)}, ...), branch_computations={%region_3.3_spmd, %region_4.6_spmd} | conditional | flops 1098915840 | bytes 54526076 | solution.py:93
  162.1 1.9 fusion.6
  164.0 1.8 fusion.10
  165.9 3.3 %multiply_add_fusion = f32[4,4,256,128]{3,2,1,0:T(8,128)S(1)} fusion(f32[4,4,256,128]{3,2,1,0:T(8,128)S(1)} %copy-done, bf16[512,4,128,1]{0,2,3,1:T(8,128)(2,1)S(1)} %bitcast.89, f32[4,512,256,4]{2,1,3,0:T(8,128)S(1)} %get-tuple-element.543, f32[4,4,256]{2,1,0:T(4,128)S(1)} %max.5, pred[4,256,512]{1,2,0:T(8,128)(4,1)S(1)} %and_or_fusion, ...), kind=kOutput, calls=%fused_computation.16 | convolution fusion | flops 546308096 | bytes 13664256 | tf_op jit(solution)/shard_map/while/body/eval_jaxpr/cond/branch_1_fun/gjqk,kgd->gjqd/dot_general | solution.py:80
  174.3 11.1 %conditional.4 = ((f32[4,4,256]{2,1,0:T(4,128)S(1)}, f32[4,4,256]{2,1,0:T(4,128)S(1)}, f32[4,4,256,128]{3,2,1,0:T(8,128)})) conditional(s32[]{:T(128)} %convert_element_type.38, (f32[4,4,256]{2,1,0:T(4,128)S(1)}, f32[4,4,256]{2,1,0:T(4,128)S(1)}, f32[4,4,256,128]{3,2,1,0:T(8,128)}) %tuple.85, (pred[256,512]{0,1:T(8,128)(4,1)S(1)}, ...), branch_computations={%region_3.3_spmd, %region_4.6_spmd} | conditional | flops 1098915840 | bytes 54526076 | solution.py:93
  176.9 1.9 fusion.6
  178.9 1.8 fusion.10
  180.7 3.3 %multiply_add_fusion = f32[4,4,256,128]{3,2,1,0:T(8,128)S(1)} fusion(f32[4,4,256,128]{3,2,1,0:T(8,128)S(1)} %copy-done, bf16[512,4,128,1]{0,2,3,1:T(8,128)(2,1)S(1)} %bitcast.89, f32[4,512,256,4]{2,1,3,0:T(8,128)S(1)} %get-tuple-element.543, f32[4,4,256]{2,1,0:T(4,128)S(1)} %max.5, pred[4,256,512]{1,2,0:T(8,128)(4,1)S(1)} %and_or_fusion, ...), kind=kOutput, calls=%fused_computation.16 | convolution fusion | flops 546308096 | bytes 13664256 | tf_op jit(solution)/shard_map/while/body/eval_jaxpr/cond/branch_1_fun/gjqk,kgd->gjqd/dot_general | solution.py:80
  189.1 11.1 %conditional.4 = ((f32[4,4,256]{2,1,0:T(4,128)S(1)}, f32[4,4,256]{2,1,0:T(4,128)S(1)}, f32[4,4,256,128]{3,2,1,0:T(8,128)})) conditional(s32[]{:T(128)} %convert_element_type.38, (f32[4,4,256]{2,1,0:T(4,128)S(1)}, f32[4,4,256]{2,1,0:T(4,128)S(1)}, f32[4,4,256,128]{3,2,1,0:T(8,128)}) %tuple.85, (pred[256,512]{0,1:T(8,128)(4,1)S(1)}, ...), branch_computations={%region_3.3_spmd, %region_4.6_spmd} | conditional | flops 1098915840 | bytes 54526076 | solution.py:93
  191.8 1.9 fusion.6
  193.7 1.8 fusion.10
  195.6 3.3 %multiply_add_fusion = f32[4,4,256,128]{3,2,1,0:T(8,128)S(1)} fusion(f32[4,4,256,128]{3,2,1,0:T(8,128)S(1)} %copy-done, bf16[512,4,128,1]{0,2,3,1:T(8,128)(2,1)S(1)} %bitcast.89, f32[4,512,256,4]{2,1,3,0:T(8,128)S(1)} %get-tuple-element.543, f32[4,4,256]{2,1,0:T(4,128)S(1)} %max.5, pred[4,256,512]{1,2,0:T(8,128)(4,1)S(1)} %and_or_fusion, ...), kind=kOutput, calls=%fused_computation.16 | convolution fusion | flops 546308096 | bytes 13664256 | tf_op jit(solution)/shard_map/while/body/eval_jaxpr/cond/branch_1_fun/gjqk,kgd->gjqd/dot_general | solution.py:80
  204.0 11.1 %conditional.4 = ((f32[4,4,256]{2,1,0:T(4,128)S(1)}, f32[4,4,256]{2,1,0:T(4,128)S(1)}, f32[4,4,256,128]{3,2,1,0:T(8,128)})) conditional(s32[]{:T(128)} %convert_element_type.38, (f32[4,4,256]{2,1,0:T(4,128)S(1)}, f32[4,4,256]{2,1,0:T(4,128)S(1)}, f32[4,4,256,128]{3,2,1,0:T(8,128)}) %tuple.85, (pred[256,512]{0,1:T(8,128)(4,1)S(1)}, ...), branch_computations={%region_3.3_spmd, %region_4.6_spmd} | conditional | flops 1098915840 | bytes 54526076 | solution.py:93
  206.6 1.9 fusion.6
  210.4 3.3 %multiply_add_fusion = f32[4,4,256,128]{3,2,1,0:T(8,128)S(1)} fusion(f32[4,4,256,128]{3,2,1,0:T(8,128)S(1)} %copy-done, bf16[512,4,128,1]{0,2,3,1:T(8,128)(2,1)S(1)} %bitcast.89, f32[4,512,256,4]{2,1,3,0:T(8,128)S(1)} %get-tuple-element.543, f32[4,4,256]{2,1,0:T(4,128)S(1)} %max.5, pred[4,256,512]{1,2,0:T(8,128)(4,1)S(1)} %and_or_fusion, ...), kind=kOutput, calls=%fused_computation.16 | convolution fusion | flops 546308096 | bytes 13664256 | tf_op jit(solution)/shard_map/while/body/eval_jaxpr/cond/branch_1_fun/gjqk,kgd->gjqd/dot_general | solution.py:80
  218.8 11.1 %conditional.4 = ((f32[4,4,256]{2,1,0:T(4,128)S(1)}, f32[4,4,256]{2,1,0:T(4,128)S(1)}, f32[4,4,256,128]{3,2,1,0:T(8,128)})) conditional(s32[]{:T(128)} %convert_element_type.38, (f32[4,4,256]{2,1,0:T(4,128)S(1)}, f32[4,4,256]{2,1,0:T(4,128)S(1)}, f32[4,4,256,128]{3,2,1,0:T(8,128)}) %tuple.85, (pred[256,512]{0,1:T(8,128)(4,1)S(1)}, ...), branch_computations={%region_3.3_spmd, %region_4.6_spmd} | conditional | flops 1098915840 | bytes 54526076 | solution.py:93
  221.5 1.9 fusion.6
  225.2 3.3 %multiply_add_fusion = f32[4,4,256,128]{3,2,1,0:T(8,128)S(1)} fusion(f32[4,4,256,128]{3,2,1,0:T(8,128)S(1)} %copy-done, bf16[512,4,128,1]{0,2,3,1:T(8,128)(2,1)S(1)} %bitcast.89, f32[4,512,256,4]{2,1,3,0:T(8,128)S(1)} %get-tuple-element.543, f32[4,4,256]{2,1,0:T(4,128)S(1)} %max.5, pred[4,256,512]{1,2,0:T(8,128)(4,1)S(1)} %and_or_fusion, ...), kind=kOutput, calls=%fused_computation.16 | convolution fusion | flops 546308096 | bytes 13664256 | tf_op jit(solution)/shard_map/while/body/eval_jaxpr/cond/branch_1_fun/gjqk,kgd->gjqd/dot_general | solution.py:80
  233.6 11.1 %conditional.4 = ((f32[4,4,256]{2,1,0:T(4,128)S(1)}, f32[4,4,256]{2,1,0:T(4,128)S(1)}, f32[4,4,256,128]{3,2,1,0:T(8,128)})) conditional(s32[]{:T(128)} %convert_element_type.38, (f32[4,4,256]{2,1,0:T(4,128)S(1)}, f32[4,4,256]{2,1,0:T(4,128)S(1)}, f32[4,4,256,128]{3,2,1,0:T(8,128)}) %tuple.85, (pred[256,512]{0,1:T(8,128)(4,1)S(1)}, ...), branch_computations={%region_3.3_spmd, %region_4.6_spmd} | conditional | flops 1098915840 | bytes 54526076 | solution.py:93
  236.3 1.9 fusion.6
  240.1 3.3 %multiply_add_fusion = f32[4,4,256,128]{3,2,1,0:T(8,128)S(1)} fusion(f32[4,4,256,128]{3,2,1,0:T(8,128)S(1)} %copy-done, bf16[512,4,128,1]{0,2,3,1:T(8,128)(2,1)S(1)} %bitcast.89, f32[4,512,256,4]{2,1,3,0:T(8,128)S(1)} %get-tuple-element.543, f32[4,4,256]{2,1,0:T(4,128)S(1)} %max.5, pred[4,256,512]{1,2,0:T(8,128)(4,1)S(1)} %and_or_fusion, ...), kind=kOutput, calls=%fused_computation.16 | convolution fusion | flops 546308096 | bytes 13664256 | tf_op jit(solution)/shard_map/while/body/eval_jaxpr/cond/branch_1_fun/gjqk,kgd->gjqd/dot_general | solution.py:80
  248.5 11.1 %conditional.4 = ((f32[4,4,256]{2,1,0:T(4,128)S(1)}, f32[4,4,256]{2,1,0:T(4,128)S(1)}, f32[4,4,256,128]{3,2,1,0:T(8,128)})) conditional(s32[]{:T(128)} %convert_element_type.38, (f32[4,4,256]{2,1,0:T(4,128)S(1)}, f32[4,4,256]{2,1,0:T(4,128)S(1)}, f32[4,4,256,128]{3,2,1,0:T(8,128)}) %tuple.85, (pred[256,512]{0,1:T(8,128)(4,1)S(1)}, ...), branch_computations={%region_3.3_spmd, %region_4.6_spmd} | conditional | flops 1098915840 | bytes 54526076 | solution.py:93
  251.1 1.9 fusion.6
  254.9 3.3 %multiply_add_fusion = f32[4,4,256,128]{3,2,1,0:T(8,128)S(1)} fusion(f32[4,4,256,128]{3,2,1,0:T(8,128)S(1)} %copy-done, bf16[512,4,128,1]{0,2,3,1:T(8,128)(2,1)S(1)} %bitcast.89, f32[4,512,256,4]{2,1,3,0:T(8,128)S(1)} %get-tuple-element.543, f32[4,4,256]{2,1,0:T(4,128)S(1)} %max.5, pred[4,256,512]{1,2,0:T(8,128)(4,1)S(1)} %and_or_fusion, ...), kind=kOutput, calls=%fused_computation.16 | convolution fusion | flops 546308096 | bytes 13664256 | tf_op jit(solution)/shard_map/while/body/eval_jaxpr/cond/branch_1_fun/gjqk,kgd->gjqd/dot_general | solution.py:80
  259.6 1.9 fusion.24
  (230 shorter events, 103.4 us)
Async XLA Ops:
  6.5 126.4 %all-gather.2.cloned.1.call-start = ((), (), s32[]{:S(2)}) async-start(), calls=%async_computation.2 | async-start | bytes 4456448 | tf_op jit(solution)/shard_map/all_gather | solution.py:98
  23.0 11.4 %collective-permute-start = (bf16[256,512]{1,0:T(8,128)(2,1)S(1)}, bf16[256,512]{1,0:T(8,128)(2,1)S(1)}, u32[]{:S(2)}, u32[]{:S(2)}) collective-permute-start(bf16[256,512]{1,0:T(8,128)(2,1)S(1)} %bitcast.95), channel_id=1, source_target_pairs={{0,2},{2,4},{4,6},{6,8},{8,10},{10,12},{12,14},{14,16},{16,18},{18... | collective-permute-start | bytes 786440 | tf_op jit(solution)/shard_map/ppermute | solution.py:28
  34.3 8.5 %collective-permute-start.1 = (bf16[256,512]{1,0:T(8,128)(2,1)S(1)}, bf16[256,512]{1,0:T(8,128)(2,1)S(1)}, u32[]{:S(2)}, u32[]{:S(2)}) collective-permute-start(bf16[256,512]{1,0:T(8,128)(2,1)S(1)} %collective-permute-done), channel_id=1, source_target_pairs={{0,2},{2,4},{4,6},{6,8},{8,10},{10,12},{12,14},{14,16},{16,18},{18... | collective-permute-start | bytes 786440 | tf_op jit(solution)/shard_map/ppermute | solution.py:28
  39.5 9.9 %collective-permute-start.8 = (bf16[256,512]{1,0:T(8,128)(2,1)S(1)}, bf16[256,512]{1,0:T(8,128)(2,1)S(1)}, u32[]{:S(2)}, u32[]{:S(2)}) collective-permute-start(bf16[256,512]{1,0:T(8,128)(2,1)S(1)} %bitcast.96), channel_id=1, source_target_pairs={{2,0},{4,2},{6,4},{8,6},{10,8},{12,10},{14,12},{16,14},{18,16},{20... | collective-permute-start | bytes 786440 | tf_op jit(solution)/shard_map/ppermute | solution.py:30
  42.8 14.1 %collective-permute-start.2 = (bf16[256,512]{1,0:T(8,128)(2,1)S(1)}, bf16[256,512]{1,0:T(8,128)(2,1)S(1)}, u32[]{:S(2)}, u32[]{:S(2)}) collective-permute-start(bf16[256,512]{1,0:T(8,128)(2,1)S(1)} %collective-permute-done.1), channel_id=1, source_target_pairs={{0,2},{2,4},{4,6},{6,8},{8,10},{10,12},{12,14},{14,16},{16,18},{18... | collective-permute-start | bytes 786440 | tf_op jit(solution)/shard_map/ppermute | solution.py:28
  49.4 12.7 %collective-permute-start.9 = (bf16[256,512]{1,0:T(8,128)(2,1)S(1)}, bf16[256,512]{1,0:T(8,128)(2,1)S(1)}, u32[]{:S(2)}, u32[]{:S(2)}) collective-permute-start(bf16[256,512]{1,0:T(8,128)(2,1)S(1)} %collective-permute-done.8), channel_id=1, source_target_pairs={{2,0},{4,2},{6,4},{8,6},{10,8},{12,10},{14,12},{16,14},{18,16},{20... | collective-permute-start | bytes 786440 | tf_op jit(solution)/shard_map/ppermute | solution.py:30
  56.9 43.8 %copy-start.2 = (bf16[256,512]{1,0:T(8,128)(2,1)}, bf16[256,512]{1,0:T(8,128)(2,1)S(1)}, u32[]{:S(2)}) copy-start(bf16[256,512]{1,0:T(8,128)(2,1)S(1)} %collective-permute-done.2) | copy-start | bytes 786436
  56.9 9.9 %collective-permute-start.3 = (bf16[256,512]{1,0:T(8,128)(2,1)S(1)}, bf16[256,512]{1,0:T(8,128)(2,1)S(1)}, u32[]{:S(2)}, u32[]{:S(2)}) collective-permute-start(bf16[256,512]{1,0:T(8,128)(2,1)S(1)} %collective-permute-done.2), channel_id=1, source_target_pairs={{0,2},{2,4},{4,6},{6,8},{8,10},{10,12},{12,14},{14,16},{16,18},{18... | collective-permute-start | bytes 786440 | tf_op jit(solution)/shard_map/ppermute | solution.py:28
  62.1 12.2 %collective-permute-start.10 = (bf16[256,512]{1,0:T(8,128)(2,1)S(1)}, bf16[256,512]{1,0:T(8,128)(2,1)S(1)}, u32[]{:S(2)}, u32[]{:S(2)}) collective-permute-start(bf16[256,512]{1,0:T(8,128)(2,1)S(1)} %collective-permute-done.9), channel_id=1, source_target_pairs={{2,0},{4,2},{6,4},{8,6},{10,8},{12,10},{14,12},{16,14},{18,16},{20... | collective-permute-start | bytes 786440 | tf_op jit(solution)/shard_map/ppermute | solution.py:30
  66.9 33.9 %copy-start.7 = (bf16[256,512]{1,0:T(8,128)(2,1)}, bf16[256,512]{1,0:T(8,128)(2,1)S(1)}, u32[]{:S(2)}) copy-start(bf16[256,512]{1,0:T(8,128)(2,1)S(1)} %collective-permute-done.3) | copy-start | bytes 786436
  66.9 9.2 %collective-permute-start.4 = (bf16[256,512]{1,0:T(8,128)(2,1)S(1)}, bf16[256,512]{1,0:T(8,128)(2,1)S(1)}, u32[]{:S(2)}, u32[]{:S(2)}) collective-permute-start(bf16[256,512]{1,0:T(8,128)(2,1)S(1)} %collective-permute-done.3), channel_id=1, source_target_pairs={{0,2},{2,4},{4,6},{6,8},{8,10},{10,12},{12,14},{14,16},{16,18},{18... | collective-permute-start | bytes 786440 | tf_op jit(solution)/shard_map/ppermute | solution.py:28
  74.3 26.5 %copy-start.3 = (bf16[256,512]{1,0:T(8,128)(2,1)}, bf16[256,512]{1,0:T(8,128)(2,1)S(1)}, u32[]{:S(2)}) copy-start(bf16[256,512]{1,0:T(8,128)(2,1)S(1)} %collective-permute-done.10) | copy-start | bytes 786436
  74.3 8.6 %collective-permute-start.11 = (bf16[256,512]{1,0:T(8,128)(2,1)S(1)}, bf16[256,512]{1,0:T(8,128)(2,1)S(1)}, u32[]{:S(2)}, u32[]{:S(2)}) collective-permute-start(bf16[256,512]{1,0:T(8,128)(2,1)S(1)} %collective-permute-done.10), channel_id=1, source_target_pairs={{2,0},{4,2},{6,4},{8,6},{10,8},{12,10},{14,12},{16,14},{18,16},{20... | collective-permute-start | bytes 786440 | tf_op jit(solution)/shard_map/ppermute | solution.py:30
  76.0 15.6 %copy-start.8 = (bf16[256,512]{1,0:T(8,128)(2,1)}, bf16[256,512]{1,0:T(8,128)(2,1)S(1)}, u32[]{:S(2)}) copy-start(bf16[256,512]{1,0:T(8,128)(2,1)S(1)} %collective-permute-done.4) | copy-start | bytes 786436
  76.0 8.6 %collective-permute-start.5 = (bf16[256,512]{1,0:T(8,128)(2,1)S(1)}, bf16[256,512]{1,0:T(8,128)(2,1)S(1)}, u32[]{:S(2)}, u32[]{:S(2)}) collective-permute-start(bf16[256,512]{1,0:T(8,128)(2,1)S(1)} %collective-permute-done.4), channel_id=1, source_target_pairs={{0,2},{2,4},{4,6},{6,8},{8,10},{10,12},{12,14},{14,16},{16,18},{18... | collective-permute-start | bytes 786440 | tf_op jit(solution)/shard_map/ppermute | solution.py:28
  82.9 17.9 %copy-start.5 = (bf16[256,512]{1,0:T(8,128)(2,1)}, bf16[256,512]{1,0:T(8,128)(2,1)S(1)}, u32[]{:S(2)}) copy-start(bf16[256,512]{1,0:T(8,128)(2,1)S(1)} %collective-permute-done.11) | copy-start | bytes 786436
  82.9 8.7 %collective-permute-start.12 = (bf16[256,512]{1,0:T(8,128)(2,1)S(1)}, bf16[256,512]{1,0:T(8,128)(2,1)}, u32[]{:S(2)}, u32[]{:S(2)}) collective-permute-start(bf16[256,512]{1,0:T(8,128)(2,1)S(1)} %collective-permute-done.11), channel_id=1, source_target_pairs={{2,0},{4,2},{6,4},{8,6},{10,8},{12,10},{14,12},{16,14},{18,16},{20... | collective-permute-start | bytes 786440 | tf_op jit(solution)/shard_map/ppermute | solution.py:30
  84.6 7.0 %copy-start.9 = (bf16[256,512]{1,0:T(8,128)(2,1)}, bf16[256,512]{1,0:T(8,128)(2,1)S(1)}, u32[]{:S(2)}) copy-start(bf16[256,512]{1,0:T(8,128)(2,1)S(1)} %collective-permute-done.5) | copy-start | bytes 786436
  84.6 8.6 %collective-permute-start.6 = (bf16[256,512]{1,0:T(8,128)(2,1)S(1)}, bf16[256,512]{1,0:T(8,128)(2,1)}, u32[]{:S(2)}, u32[]{:S(2)}) collective-permute-start(bf16[256,512]{1,0:T(8,128)(2,1)S(1)} %collective-permute-done.5), channel_id=1, source_target_pairs={{0,2},{2,4},{4,6},{6,8},{8,10},{10,12},{12,14},{14,16},{16,18},{18... | collective-permute-start | bytes 786440 | tf_op jit(solution)/shard_map/ppermute | solution.py:28
  91.6 9.9 %collective-permute-start.13 = (bf16[256,512]{1,0:T(8,128)(2,1)}, bf16[256,512]{1,0:T(8,128)(2,1)}, u32[]{:S(2)}, u32[]{:S(2)}) collective-permute-start(bf16[256,512]{1,0:T(8,128)(2,1)} %collective-permute-done.12), channel_id=1, source_target_pairs={{2,0},{4,2},{6,4},{8,6},{10,8},{12,10},{14,12},{16,14},{18,16},{20... | collective-permute-start | bytes 786440 | tf_op jit(solution)/shard_map/ppermute | solution.py:30
  93.2 8.9 %collective-permute-start.7 = (bf16[256,512]{1,0:T(8,128)(2,1)}, bf16[256,512]{1,0:T(8,128)(2,1)}, u32[]{:S(2)}, u32[]{:S(2)}) collective-permute-start(bf16[256,512]{1,0:T(8,128)(2,1)} %collective-permute-done.6), channel_id=1, source_target_pairs={{0,2},{2,4},{4,6},{6,8},{8,10},{10,12},{12,14},{14,16},{16,18},{18... | collective-permute-start | bytes 786440 | tf_op jit(solution)/shard_map/ppermute | solution.py:28
  101.5 14.3 %copy-start.4 = (bf16[256,512]{1,0:T(8,128)(2,1)S(1)}, bf16[256,512]{1,0:T(8,128)(2,1)}, u32[]{:S(2)}) copy-start(bf16[256,512]{1,0:T(8,128)(2,1)} %copy-done.3) | copy-start | bytes 786436
  101.5 15.0 %copy-start.6 = (bf16[256,512]{1,0:T(8,128)(2,1)S(1)}, bf16[256,512]{1,0:T(8,128)(2,1)}, u32[]{:S(2)}) copy-start(bf16[256,512]{1,0:T(8,128)(2,1)} %copy-done.5) | copy-start | bytes 786436
  101.6 19.1 %collective-permute-start.14 = (bf16[256,512]{1,0:T(8,128)(2,1)}, bf16[256,512]{1,0:T(8,128)(2,1)S(1)}, u32[]{:S(2)}, u32[]{:S(2)}) collective-permute-start(bf16[256,512]{1,0:T(8,128)(2,1)} %collective-permute-done.13), channel_id=1, source_target_pairs={{2,0},{4,2},{6,4},{8,6},{10,8},{12,10},{14,12},{16,14},{18,16},{20... | collective-permute-start | bytes 786440 | tf_op jit(solution)/shard_map/ppermute | solution.py:30
  149.2 1.9 copy-start
  154.4 1.3 copy-start.1
  164.0 1.9 copy-start
  169.2 1.3 copy-start.1
  178.8 1.9 copy-start
  184.1 1.3 copy-start.1
  193.7 1.9 copy-start
  198.9 1.3 copy-start.1
  208.5 1.9 copy-start
  213.7 1.3 copy-start.1
  223.4 1.9 copy-start
  228.6 1.3 copy-start.1
  238.2 1.9 copy-start
  243.4 1.3 copy-start.1
  253.0 1.9 copy-start
  258.2 1.3 copy-start.1
Sparse Core Ops, SparseCore 0:
  15.4 62.5 all-gather.1
